TPU v7x, 32 devices: a whole 2x2x4 slice. The times are simulated.
32 devices in a mesh: grp: 4 (over y, x), mem: 8 (over z, core).
Axes of the slice: x: 2, y: 2, z: 4, core: 2. Of those that a mesh axis runs over, the one named last changes fastest.
Arguments:
- factors: bfloat16 [32, 512, 2048], P(('grp', 'mem')), may hold values from -1 to 1
- occ_energy: bfloat16 [32], P(('grp', 'mem')), may hold values from -1.5 to -0.29882812
- vir_energy: bfloat16 [512], replicated, may hold values from 0.3984375 to 3
- pair_code: int32 [4, 8, 3], P('grp'), may hold values from 0 to 2
- pair_count: int32 [4, 8], P('grp'), may hold values from 1 to 3
Outputs:
- aux_density: bfloat16 [32, 512, 2048], P(('grp', 'mem'))
- lagrangian: bfloat16 [32, 512, 2048], P(('grp', 'mem'))
Inputs may be any that keep to these rules, and one draw needn't show every extreme that they name: `pair_code`: only the first pair_count entries of a device's list are read; entries may repeat.
All inputs are finite; a program needn't handle non-finite values.
Results may differ from a plain program's by a relative error of at most 0.0056.
Values may be sent and summed in bfloat16 or wider, within the bound.
No kernel may reach another device: no remote copies, remote signals or barrier semaphores. Data moves between devices by JAX's collectives and lax.ppermute only.
A program may use at most 128 MiB of HBM per device.

v0:
```python
import jax
import jax.numpy as jnp
from jax import lax
from jax.sharding import PartitionSpec as P

OCC_DEV = 1
ROUNDS = 2


def partner(value, axis, distance):
    mask = 2**distance
    pairs = [(source, source ^ mask) for source in range(lax.axis_size(axis))]
    return lax.ppermute(value, axis, pairs)


def decode_pair(code):
    round_no = code // (OCC_DEV * OCC_DEV)
    left_orb = code // OCC_DEV % OCC_DEV
    right_orb = code % OCC_DEV
    return (round_no, left_orb, right_orb)


def add_at(target, indices, contribution):
    zero_index = jnp.zeros((), jnp.int32)
    anchor = tuple(indices) + (zero_index,) * contribution.ndim
    extent = (1,) * len(indices) + contribution.shape
    current = lax.dynamic_slice(target, anchor, extent)
    return lax.dynamic_update_slice(target, current + contribution.reshape(extent), anchor)


def outer_terms(amp_tile):
    return lax.dot_general(
        amp_tile, amp_tile, (((1,), (1,)), ((), ())), preferred_element_type=jnp.float32
    )


def near_product(amp_tile, right_block):
    return jnp.dot(amp_tile, right_block, preferred_element_type=jnp.float32)


def far_product(amp_tile, left_block):
    return lax.dot_general(
        amp_tile, left_block, (((0,), (0,)), ((), ())), preferred_element_type=jnp.float32
    )


def per_device(factors, occ_energy, vir_energy, pair_code, pair_count):
    virtual = vir_energy.astype(jnp.float32)
    my_place = lax.axis_index("mem")
    group_codes = pair_code[0]
    group_counts = pair_count[0]
    my_codes = lax.dynamic_index_in_dim(group_codes, my_place, 0, keepdims=False)
    live_count = lax.dynamic_index_in_dim(group_counts, my_place, 0, keepdims=False)
    blocks_all = [factors]
    energy_list = [occ_energy]
    for round_idx in range(ROUNDS):
        visitor, visitor_energy = partner((factors, occ_energy), "mem", round_idx)
        blocks_all.append(visitor)
        energy_list.append(visitor_energy)
    stacked = jnp.stack(blocks_all)
    energy_all = jnp.stack(energy_list).astype(jnp.float32)
    vir_count = factors.shape[1]
    density_zero = jnp.zeros((vir_count, vir_count), jnp.float32)

    def pair_terms(slot_no):
        round_no, left_orb, right_orb = decode_pair(my_codes[slot_no])
        left_block = stacked[0, left_orb]
        right_block = stacked[round_no, right_orb]
        integrals = lax.dot_general(
            left_block, right_block, (((1,), (1,)), ((), ())), preferred_element_type=jnp.float32
        )
        denominator = (
            virtual[:, None]
            + virtual[None, :]
            - energy_all[0, left_orb]
            - energy_all[round_no, right_orb]
        )
        amp_tile = (integrals / denominator).astype(jnp.bfloat16)
        return (round_no, left_orb, right_orb, left_block, right_block, amp_tile)

    def pair_step(slot_no, carry_pair):
        density, totals = carry_pair
        round_no, left_orb, right_orb, left_block, right_block, amp_tile = pair_terms(slot_no)
        density = density + outer_terms(amp_tile)
        totals = add_at(
            totals, (jnp.zeros((), jnp.int32), left_orb), near_product(amp_tile, right_block)
        )
        totals = add_at(totals, (round_no, right_orb), far_product(amp_tile, left_block))
        return (density, totals)

    totals_zero = jnp.zeros((ROUNDS + 1,) + factors.shape, jnp.float32)
    density, totals = lax.fori_loop(0, live_count, pair_step, (density_zero, totals_zero))
    gathered = totals[0]
    for round_idx in range(ROUNDS):
        gathered = gathered + partner(totals[round_idx + 1], "mem", round_idx)
    density = lax.psum(density, "mem")
    density = lax.psum(density, "grp")
    density_scale = 1.0 / (8.0 * lax.axis_size("grp") * lax.axis_size("mem"))
    density_tile = (density * density_scale).astype(jnp.bfloat16)
    lagrangian = jnp.einsum(
        "ab,kbp->kap", density_tile, factors, preferred_element_type=jnp.float32
    )
    return (gathered.astype(jnp.bfloat16), lagrangian.astype(jnp.bfloat16))


def solution(mesh):
    in_specs = (
        P(("grp", "mem"), None, None),
        P(("grp", "mem")),
        P(),
        P("grp", None, None),
        P("grp", None),
    )
    out_specs = (P(("grp", "mem"), None, None), P(("grp", "mem"), None, None))
    return jax.shard_map(
        per_device, mesh=mesh, in_specs=in_specs, out_specs=out_specs, check_vma=False
    )
```

profile of v0, /device:TPU:0, one launch (start us, length us, event | category | flops | bytes accessed | tf_op | source)
XLA Modules:
  0.0 275.8 jit_solution(6055429350554140018)
XLA Ops:
  7.2 0.0 copy-start
  7.2 0.0 all-reduce.3.cloned.1.call-start
  7.2 0.6 collective-permute-start
  7.8 2.6 collective-permute-start.1
  10.4 0.1 collective-permute-start.3
  10.5 0.1 collective-permute-start.2
  11.3 0.7 convert_element_type.38
  11.9 1.2 constant_dynamic-slice_fusion.1
  13.2 0.2 dynamic-slice_reduce_fusion
  13.4 43.7 %collective-permute-done.3 = bf16[1]{0:T(256)(128)(2,1)} collective-permute-done((bf16[1]{0:T(256)(128)(2,1)}, bf16[1]{0:T(256)(128)(2,1)}, u32[]{:S(2)}, u32[]{:S(2)}) %collective-permute-start.3) | collective-permute-done | bytes 34 | tf_op jit(solution)/shard_map/ppermute | solution.py:13
  57.1 1.3 maximum_convert_fusion
  58.3 5.5 %pad_maximum_fusion = bf16[3,1,512,2048]{3,2,1,0:T(8,128)(2,1)} fusion(bf16[1,1,512,2048]{3,2,1,0:T(8,128)(2,1)} %bitcast.11, bf16[1,1,512,2048]{3,2,1,0:T(8,128)(2,1)S(1)} %bitcast.93, bf16[1,1,512,2048]{3,2,1,0:T(8,128)(2,1)} %bitcast.92), kind=kLoop, calls=%fused_computation.19 | loop fusion | flops 6291456 | bytes 12582912 | tf_op jit(solution)/shard_map/stack | solution.py:60
  63.8 0.1 broadcast_in_dim.8
  63.9 6.1 %broadcast_in_dim.9 = f32[3,1,512,2048]{3,2,1,0:T(8,128)} broadcast(f32[]{:T(128)} %constant.74.clone.1), dimensions={} | broadcast | bytes 12582916 | tf_op jit(solution)/shard_map/broadcast_in_dim | solution.py:91
  70.1 58.7 %while.14 = (s32[]{:T(128)}, f32[512,512]{1,0:T(8,128)S(1)}, f32[3,1,512,2048]{3,2,1,0:T(8,128)}, s32[]{:T(128)}, s32[3]{0:T(128)S(1)}, /*index=5*/bf16[3,1,512,...) while((s32[]{:T(128)}, f32[512,512]{1,0:T(8,128)S(1)}, ...), condition=%wide.region_1.2_spmd, body=%wide.region_0.1_spmd.sunk | while | flops 3493330944 | bytes 155194704 | solution.py:92
  70.7 0.6 dynamic_slice.94
  73.4 0.6 fusion.52
  74.0 6.0 %divide_convert_fusion.2 = bf16[512,512]{0,1:T(8,128)(2,1)S(1)} fusion(bf16[3,1,512,2048]{3,2,1,0:T(8,128)(2,1)} %get-tuple-element.212, s32[]{:T(128)S(6)} %select_n.46, f32[]{:T(128)} %bitcast.89, f32[]{:T(128)} %bitcast.90, f32[512]{0:T(512)S(1)} %get-tuple-element.213), kind=kOutput, calls=%fused_computation.15.clone.1 | convolution fusion | flops 1075052544 | bytes 4723716 | tf_op jit(solution)/shard_map/while/body/dot_general | solution.py:69
  80.0 0.5 convolution_add_fusion.2
  80.5 1.1 copy-done.3
  81.7 1.6 fusion.53
  83.2 1.6 fusion.54
  84.9 4.5 %copy-done.2 = f32[3,1,512,2048]{3,2,1,0:T(8,128)} copy-done((f32[3,1,512,2048]{3,2,1,0:T(8,128)}, f32[3,1,512,2048]{3,2,1,0:T(8,128)S(1)}, u32[]{:S(2)}) %copy-start.2) | copy-done | bytes 12582936 | tf_op jit(solution)/shard_map/while
  90.1 0.6 dynamic_slice.94
  92.7 0.6 fusion.52
  93.4 6.0 %divide_convert_fusion.2 = bf16[512,512]{0,1:T(8,128)(2,1)S(1)} fusion(bf16[3,1,512,2048]{3,2,1,0:T(8,128)(2,1)} %get-tuple-element.212, s32[]{:T(128)S(6)} %select_n.46, f32[]{:T(128)} %bitcast.89, f32[]{:T(128)} %bitcast.90, f32[512]{0:T(512)S(1)} %get-tuple-element.213), kind=kOutput, calls=%fused_computation.15.clone.1 | convolution fusion | flops 1075052544 | bytes 4723716 | tf_op jit(solution)/shard_map/while/body/dot_general | solution.py:69
  99.4 0.5 convolution_add_fusion.2
  99.9 1.1 copy-done.3
  101.0 1.6 fusion.53
  102.6 1.6 fusion.54
  104.2 4.5 %copy-done.2 = f32[3,1,512,2048]{3,2,1,0:T(8,128)} copy-done((f32[3,1,512,2048]{3,2,1,0:T(8,128)}, f32[3,1,512,2048]{3,2,1,0:T(8,128)S(1)}, u32[]{:S(2)}) %copy-start.2) | copy-done | bytes 12582936 | tf_op jit(solution)/shard_map/while
  109.4 0.6 dynamic_slice.94
  112.1 0.6 fusion.52
  112.7 6.0 %divide_convert_fusion.2 = bf16[512,512]{0,1:T(8,128)(2,1)S(1)} fusion(bf16[3,1,512,2048]{3,2,1,0:T(8,128)(2,1)} %get-tuple-element.212, s32[]{:T(128)S(6)} %select_n.46, f32[]{:T(128)} %bitcast.89, f32[]{:T(128)} %bitcast.90, f32[512]{0:T(512)S(1)} %get-tuple-element.213), kind=kOutput, calls=%fused_computation.15.clone.1 | convolution fusion | flops 1075052544 | bytes 4723716 | tf_op jit(solution)/shard_map/while/body/dot_general | solution.py:69
  118.7 0.5 convolution_add_fusion.2
  119.2 1.1 copy-done.3
  120.4 1.6 fusion.53
  121.9 1.6 fusion.54
  123.6 4.5 %copy-done.2 = f32[3,1,512,2048]{3,2,1,0:T(8,128)} copy-done((f32[3,1,512,2048]{3,2,1,0:T(8,128)}, f32[3,1,512,2048]{3,2,1,0:T(8,128)S(1)}, u32[]{:S(2)}) %copy-start.2) | copy-done | bytes 12582936 | tf_op jit(solution)/shard_map/while
  128.8 8.2 %slice_bitcast_fusion.1 = (f32[1,512,2048]{2,1,0:T(8,128)}, f32[1,512,2048]{2,1,0:T(8,128)}) fusion(f32[3,1,512,2048]{3,2,1,0:T(8,128)} %get-tuple-element.109), kind=kLoop, calls=%fused_computation.24 | loop fusion | bytes 16777216 | tf_op jit(solution)/shard_map/squeeze | solution.py:95
  137.0 1.7 collective-permute-start.5
  138.8 0.0 all-reduce.3.cloned.1.call-update
  138.8 0.0 all-reduce.5.cloned.1.call-start
  138.8 64.7 %all-reduce.3.cloned.1.call-done = f32[512,512]{1,0:T(8,128)} async-done(((f32[512,512]{1,0:T(8,128)}), f32[512,512]{1,0:T(8,128)}) %all-reduce.3.cloned.1.call-update) | async-done | bytes 1048592 | tf_op jit(solution)/shard_map/psum | solution.py:96
  203.5 0.0 all-reduce.5.cloned.1.call-update
  203.5 54.6 %all-reduce.5.cloned.1.call-done = f32[512,512]{1,0:T(8,128)} async-done(((f32[512,512]{1,0:T(8,128)}), f32[512,512]{1,0:T(8,128)}) %all-reduce.5.cloned.1.call-update) | async-done | bytes 1048592 | tf_op jit(solution)/shard_map/psum | solution.py:97
  258.1 3.8 %fusion.24 = bf16[1,512,2048]{2,1,0:T(8,128)(2,1)} fusion(bf16[1,512,2048]{2,1,0:T(8,128)(2,1)S(1)} %copy-done.5, f32[512,512]{1,0:T(8,128)} %all-reduce.5.cloned.1.call-done), kind=kOutput, calls=%fused_computation.26 | convolution fusion | flops 1075314688 | bytes 5242880 | tf_op jit(solution)/shard_map/ab,kbp->kap/dot_general | solution.py:100
  261.9 7.1 %fusion.23 = bf16[1,512,2048]{2,1,0:T(8,128)(2,1)} fusion(f32[1,512,2048]{2,1,0:T(8,128)} %collective-permute-done.5, f32[1,512,2048]{2,1,0:T(8,128)} %collective-permute-done.4, f32[3,1,512,2048]{3,2,1,0:T(8,128)} %get-tuple-element.109), kind=kLoop, calls=%fused_computation.22 | loop fusion | flops 3145728 | bytes 14680064 | tf_op jit(solution)/shard_map/convert_element_type | solution.py:103
  (23 shorter events, 0.1 us)
Async XLA Ops:
  7.2 6.0 %copy-start = (s32[1,8,3]{1,0,2:T(1,128)S(1)}, s32[1,8,3]{1,0,2:T(1,128)}, u32[]{:S(2)}) copy-start(s32[1,8,3]{1,0,2:T(1,128)} %param.10) | copy-start | bytes 292
  7.2 196.3 %all-reduce.3.cloned.1.call-start = ((), (), s32[]{:S(2)}) async-start(), calls=%async_computation | async-start | bytes 2097152 | tf_op jit(solution)/shard_map/psum | solution.py:96
  7.2 51.1 %collective-permute-start = (bf16[1,512,2048]{2,1,0:T(8,128)(2,1)}, bf16[1,512,2048]{2,1,0:T(8,128)(2,1)S(1)}, u32[]{:S(2)}, u32[]{:S(2)}) collective-permute-start(bf16[1,512,2048]{2,1,0:T(8,128)(2,1)} %param.7), channel_id=1, source_target_pairs={{0,1},{1,0},{2,3},{3,2},{4,5},{5,4},{6,7},{7,6},{8,9},{9,8},{10,11... | collective-permute-start | bytes 6291464 | tf_op jit(solution)/shard_map/ppermute | solution.py:13
  7.8 50.5 %collective-permute-start.1 = (bf16[1,512,2048]{2,1,0:T(8,128)(2,1)}, bf16[1,512,2048]{2,1,0:T(8,128)(2,1)}, u32[]{:S(2)}, u32[]{:S(2)}) collective-permute-start(bf16[1,512,2048]{2,1,0:T(8,128)(2,1)} %param.7), channel_id=1, source_target_pairs={{0,2},{1,3},{2,0},{3,1},{4,6},{5,7},{6,4},{7,5},{8,10},{9,11},{10,... | collective-permute-start | bytes 6291464 | tf_op jit(solution)/shard_map/ppermute | solution.py:13
  10.4 46.6 %collective-permute-start.3 = (bf16[1]{0:T(256)(128)(2,1)}, bf16[1]{0:T(256)(128)(2,1)}, u32[]{:S(2)}, u32[]{:S(2)}) collective-permute-start(bf16[1]{0:T(256)(128)(2,1)} %param.8), channel_id=1, source_target_pairs={{0,2},{1,3},{2,0},{3,1},{4,6},{5,7},{6,4},{7,5},{8,10},{9,11},{10,... | collective-permute-start | bytes 14 | tf_op jit(solution)/shard_map/ppermute | solution.py:13
  10.5 46.6 %collective-permute-start.2 = (bf16[1]{0:T(256)(128)(2,1)}, bf16[1]{0:T(256)(128)(2,1)}, u32[]{:S(2)}, u32[]{:S(2)}) collective-permute-start(bf16[1]{0:T(256)(128)(2,1)} %param.8), channel_id=1, source_target_pairs={{0,1},{1,0},{2,3},{3,2},{4,5},{5,4},{6,7},{7,6},{8,9},{9,8},{10,11... | collective-permute-start | bytes 14 | tf_op jit(solution)/shard_map/ppermute | solution.py:13
  74.0 6.5 %copy-start.1 = (f32[3,1,512,2048]{3,2,1,0:T(8,128)S(1)}, f32[3,1,512,2048]{3,2,1,0:T(8,128)}, u32[]{:S(2)}) copy-start(f32[3,1,512,2048]{3,2,1,0:T(8,128)} %get-tuple-element.198) | copy-start | bytes 37748740 | tf_op jit(solution)/shard_map/while
  74.0 7.6 %copy-start.3 = (bf16[3,1,512,2048]{3,2,1,0:T(8,128)(2,1)S(1)}, bf16[3,1,512,2048]{3,2,1,0:T(8,128)(2,1)}, u32[]{:S(2)}) copy-start(bf16[3,1,512,2048]{3,2,1,0:T(8,128)(2,1)} %get-tuple-element.212) | copy-start | bytes 18874372 | tf_op jit(solution)/shard_map/while
  84.9 4.5 %copy-start.2 = (f32[3,1,512,2048]{3,2,1,0:T(8,128)}, f32[3,1,512,2048]{3,2,1,0:T(8,128)S(1)}, u32[]{:S(2)}) copy-start(f32[3,1,512,2048]{3,2,1,0:T(8,128)S(1)} %fusion.54) | copy-start | bytes 37748740 | tf_op jit(solution)/shard_map/while
  93.4 6.5 %copy-start.1 = (f32[3,1,512,2048]{3,2,1,0:T(8,128)S(1)}, f32[3,1,512,2048]{3,2,1,0:T(8,128)}, u32[]{:S(2)}) copy-start(f32[3,1,512,2048]{3,2,1,0:T(8,128)} %get-tuple-element.198) | copy-start | bytes 37748740 | tf_op jit(solution)/shard_map/while
  93.4 7.6 %copy-start.3 = (bf16[3,1,512,2048]{3,2,1,0:T(8,128)(2,1)S(1)}, bf16[3,1,512,2048]{3,2,1,0:T(8,128)(2,1)}, u32[]{:S(2)}) copy-start(bf16[3,1,512,2048]{3,2,1,0:T(8,128)(2,1)} %get-tuple-element.212) | copy-start | bytes 18874372 | tf_op jit(solution)/shard_map/while
  104.2 4.5 %copy-start.2 = (f32[3,1,512,2048]{3,2,1,0:T(8,128)}, f32[3,1,512,2048]{3,2,1,0:T(8,128)S(1)}, u32[]{:S(2)}) copy-start(f32[3,1,512,2048]{3,2,1,0:T(8,128)S(1)} %fusion.54) | copy-start | bytes 37748740 | tf_op jit(solution)/shard_map/while
  112.7 6.5 %copy-start.1 = (f32[3,1,512,2048]{3,2,1,0:T(8,128)S(1)}, f32[3,1,512,2048]{3,2,1,0:T(8,128)}, u32[]{:S(2)}) copy-start(f32[3,1,512,2048]{3,2,1,0:T(8,128)} %get-tuple-element.198) | copy-start | bytes 37748740 | tf_op jit(solution)/shard_map/while
  112.7 7.6 %copy-start.3 = (bf16[3,1,512,2048]{3,2,1,0:T(8,128)(2,1)S(1)}, bf16[3,1,512,2048]{3,2,1,0:T(8,128)(2,1)}, u32[]{:S(2)}) copy-start(bf16[3,1,512,2048]{3,2,1,0:T(8,128)(2,1)} %get-tuple-element.212) | copy-start | bytes 18874372 | tf_op jit(solution)/shard_map/while
  123.6 4.5 %copy-start.2 = (f32[3,1,512,2048]{3,2,1,0:T(8,128)}, f32[3,1,512,2048]{3,2,1,0:T(8,128)S(1)}, u32[]{:S(2)}) copy-start(f32[3,1,512,2048]{3,2,1,0:T(8,128)S(1)} %fusion.54) | copy-start | bytes 37748740 | tf_op jit(solution)/shard_map/while
  128.8 8.3 %copy-start.4 = (f32[512,512]{1,0:T(8,128)}, f32[512,512]{1,0:T(8,128)S(1)}, u32[]{:S(2)}) copy-start(f32[512,512]{1,0:T(8,128)S(1)} %get-tuple-element.110) | copy-start | bytes 3145732
  128.8 129.3 %copy-start.5 = (bf16[1,512,2048]{2,1,0:T(8,128)(2,1)S(1)}, bf16[1,512,2048]{2,1,0:T(8,128)(2,1)}, u32[]{:S(2)}) copy-start(bf16[1,512,2048]{2,1,0:T(8,128)(2,1)} %param.7) | copy-start | bytes 6291460
  137.0 124.9 %collective-permute-start.4 = (f32[1,512,2048]{2,1,0:T(8,128)}, f32[1,512,2048]{2,1,0:T(8,128)}, u32[]{:S(2)}, u32[]{:S(2)}) collective-permute-start(f32[1,512,2048]{2,1,0:T(8,128)} %get-tuple-element.129), channel_id=1, source_target_pairs={{0,1},{1,0},{2,3},{3,2},{4,5},{5,4},{6,7},{7,6},{8,9},{9,8},{10,11... | collective-permute-start | bytes 12582920 | tf_op jit(solution)/shard_map/ppermute | solution.py:13
  137.0 124.9 %collective-permute-start.5 = (f32[1,512,2048]{2,1,0:T(8,128)}, f32[1,512,2048]{2,1,0:T(8,128)}, u32[]{:S(2)}, u32[]{:S(2)}) collective-permute-start(f32[1,512,2048]{2,1,0:T(8,128)} %get-tuple-element.130), channel_id=1, source_target_pairs={{0,2},{1,3},{2,0},{3,1},{4,6},{5,7},{6,4},{7,5},{8,10},{9,11},{10,... | collective-permute-start | bytes 12582920 | tf_op jit(solution)/shard_map/ppermute | solution.py:13
  138.8 119.3 %all-reduce.5.cloned.1.call-start = ((), (), s32[]{:S(2)}) async-start(), calls=%async_computation.1 | async-start | bytes 2097152 | tf_op jit(solution)/shard_map/psum | solution.py:97
Sparse Core Ops, SparseCore 0:
  138.9 64.5 all-reduce.2
  206.5 51.4 all-reduce.4
where the time goes:
time: 276 us
  waiting for transfers between devices  163 us (59%)
  local copies, waits for them, and re-layouts  36.8 us (13%)
  matrix products  32.8 us (12%)
  between operations  14.7 us (5%)
  other arithmetic  14.5 us (5%)
  loops' own time  8.85 us (3%)
  starting transfers between devices  5.17 us (2%)
    psum x1, waiting for transfers between devices, per_device(): density = lax.psum(density, 'mem')  64.7 us
    psum x1, waiting for transfers between devices, per_device(): density = lax.psum(density, 'grp')  54.6 us
    ppermute x6, waiting for transfers between devices, partner(): return lax.ppermute(value, axis, pairs)  43.7 us
    dot_general x3, matrix products, pair_terms(): lax.dot_general(left_block, right_block, (((1,), (1,)), ((), ())), prefer...  18 us
    while x18, local copies, waits for them, and re-layouts  17 us
    another operation x1, loops' own time, per_device(): lax.fori_loop(0, live_count, pair_step, (density_zero, totals_zero))  8.85 us
    squeeze x1, local copies, waits for them, and re-layouts, per_device(): gathered = gathered + partner(totals[round_idx + 1], 'mem', round_idx)  8.24 us
    convert_element_type x1, other arithmetic, per_device(): return (gathered.astype(jnp.bfloat16), lagrangian.astype(jnp.bfloat16))  7.07 us
  transfers between devices with their start and end apart: 8, of which 3 were waited for; matrix products, arithmetic and copies ran while one was open for 3% of the time, Pallas kernels for 0%

commit v1 on v0

v1 whole, which is shorter than its diff:
```python
import functools

import jax
import jax.numpy as jnp
from jax import lax
from jax.experimental import pallas as pl
from jax.experimental.pallas import tpu as pltpu
from jax.sharding import PartitionSpec as P

CHUNKS = 4
TILE = 128
F32 = jnp.float32
BF16 = jnp.bfloat16

VMEM = pl.BlockSpec(memory_space=pltpu.VMEM)
SMEM = pl.BlockSpec(memory_space=pltpu.SMEM)


def leads(member):
    return (member & 1) == ((member >> 1) & 1)


def first_round(member):
    return jnp.where(leads(member), 2, 1)


def turn(value, back):
    pairs = []
    for member in range(lax.axis_size("mem")):
        target = member ^ (1 if leads(member) else 2)
        pairs.append((target, member) if back else (member, target))
    return lax.ppermute(value, "mem", pairs)


def swap(value, grp_mask, mem_mask):
    groups, members = lax.axis_size("grp"), lax.axis_size("mem")
    pairs = []
    for g in range(groups):
        for m in range(members):
            mask = grp_mask(m) if callable(grp_mask) else grp_mask
            pairs.append((g * members + m, (g ^ mask) * members + (m ^ mem_mask)))
    return lax.ppermute(value, ("grp", "mem"), pairs)


def live(codes, counts, member, round_no):
    total = jnp.int32(0)
    for slot in range(codes.shape[2]):
        hit = (slot < counts[0, member]) & (codes[0, member, slot] == round_no)
        total = total + hit.astype(jnp.int32)
    return total


def weights(codes, counts, round_no):
    me = lax.axis_index("mem")
    other = jnp.where(round_no == 0, me, me ^ round_no)
    own = live(codes, counts, me, round_no)
    far = live(codes, counts, other, round_no)
    return own.astype(F32), far.astype(F32)


def nt(a, b):
    return lax.dot_general(a, b, (((1,), (1,)), ((), ())), preferred_element_type=F32)


def nn(a, b):
    return jnp.dot(a, b, preferred_element_type=F32)


def early_kernel(b_ref, row_ref, e_ref, codes, counts, base_ref, dens_ref, gamma_ref, amp):
    vir = b_ref.shape[0]
    row = row_ref[...]
    col = jnp.broadcast_to(row, (vir, vir)).T
    base_ref[...] = col + row
    own, _ = weights(codes, counts, 0)
    energy = e_ref[0]
    width = vir // CHUNKS
    for c in range(CHUNKS):
        at = pl.ds(c * width, width)
        k = nt(b_ref[...], b_ref[at, :])
        amp[:, at] = (k / (base_ref[:, at] - energy - energy)).astype(BF16)
    a = amp[...]
    dens_ref[...] = own * nn(a, a)
    for c in range(CHUNKS):
        wide = b_ref.shape[1] // CHUNKS
        at = pl.ds(c * wide, wide)
        gamma_ref[:, at] = (2.0 * own) * nn(a, b_ref[:, at])


def amp_part(b_ref, r_ref, base_ref, e_ref, far_ref, at):
    k = nt(b_ref[...], r_ref[...])
    return (k / (base_ref[:, at] - e_ref[0] - far_ref[0])).astype(BF16)


def part_kernel(part, b_ref, r_ref, base_ref, e_ref, far_ref, mt_ref, m_ref):
    width = r_ref.shape[0]
    mt = amp_part(b_ref, r_ref, base_ref, e_ref, far_ref, pl.ds(part * width, width))
    mt_ref[...] = mt
    m_ref[...] = mt.T


def blocks(size):
    count = size // TILE
    return [(i, j) for i in range(count) for j in range(i, count)]


def density_kernel(*refs):
    (b_ref, r_ref, base_ref, e_ref, far_ref, codes, counts, dens_ref), rest = refs[:8], refs[8:]
    old, (mt_ref, m_ref, keep_ref, send_ref, mt_all, m_all, packed) = rest[:-7], rest[-7:]
    width = r_ref.shape[0]
    vir = b_ref.shape[0]
    last = CHUNKS - 1
    at = pl.ds(last * width, width)
    mt = amp_part(b_ref, r_ref, base_ref, e_ref, far_ref, at)
    m = mt.T
    mt_ref[...] = mt
    m_ref[...] = m
    for c in range(last):
        mt_all[:, pl.ds(c * width, width)] = old[2 * c][...]
        m_all[pl.ds(c * width, width), :] = old[2 * c + 1][...]
    mt_all[:, at] = mt
    m_all[at, :] = m
    me = lax.axis_index("mem")
    own, far = weights(codes, counts, first_round(me))
    total = dens_ref[...] + own * nn(mt_all[...], m_all[...]) + far * nn(m_all[...], mt_all[...])
    for n, (i, j) in enumerate(blocks(vir)):
        packed[pl.ds(n * TILE, TILE), :] = total[i * TILE : (i + 1) * TILE, j * TILE : (j + 1) * TILE]
    half = keep_ref.shape[0]
    lead = leads(me).astype(jnp.int32)
    keep_ref[...] = packed[pl.ds(pl.multiple_of((1 - lead) * half, TILE), half), :]
    send_ref[...] = packed[pl.ds(pl.multiple_of(lead * half, TILE), half), :].astype(BF16)


def first_gamma_kernel(*refs):
    codes, counts, gamma_in, rest, gamma_ref = refs[0], refs[1], refs[2], refs[3:-1], refs[-1]
    own, far = weights(codes, counts, first_round(lax.axis_index("mem")))
    weight = own + far
    wide = gamma_ref.shape[1] // CHUNKS
    for p in range(CHUNKS):
        at = pl.ds(p * wide, wide)
        total = nn(rest[0][...], rest[CHUNKS][:, at])
        for c in range(1, CHUNKS):
            total = total + nn(rest[c][...], rest[CHUNKS + c][:, at])
        gamma_ref[:, at] = gamma_in[:, at] + weight * total


def second_gamma_kernel(part, codes, counts, b_ref, r_ref, base_ref, e_ref, far_ref, gamma_in, gamma_ref):
    me = lax.axis_index("mem")
    own, far = weights(codes, counts, 3 - first_round(me))
    weight = own + far
    width = r_ref.shape[0]
    mt = amp_part(b_ref, r_ref, base_ref, e_ref, far_ref, pl.ds(part * width, width))
    wide = gamma_ref.shape[1] // CHUNKS
    for p in range(CHUNKS):
        at = pl.ds(p * wide, wide)
        total = gamma_in[:, at] + weight * nn(mt, r_ref[:, at])
        gamma_ref[:, at] = total.astype(gamma_ref.dtype)


def apply_kernel(mine_ref, other_ref, b_ref, out_ref, tile):
    vir = tile.shape[0]

    @pl.when(pl.program_id(0) == 0)
    def _():
        lead = leads(lax.axis_index("mem"))
        names = blocks(vir)
        half = len(names) // 2
        for n, (i, j) in enumerate(names):
            at = pl.ds((n % half) * TILE, TILE)
            low, high = (mine_ref, other_ref) if n < half else (other_ref, mine_ref)
            block = jnp.where(lead, low[at, :].astype(F32), high[at, :].astype(F32))
            tile[pl.ds(i * TILE, TILE), pl.ds(j * TILE, TILE)] = block.astype(BF16)
            if i != j:
                tile[pl.ds(j * TILE, TILE), pl.ds(i * TILE, TILE)] = block.T.astype(BF16)

    out_ref[...] = nn(tile[...], b_ref[...]).astype(BF16)


def call(kernel, outs, scratch=(), smem=(), count=0, flops=0, name=None):
    return pl.pallas_call(
        kernel,
        out_shape=outs,
        in_specs=[SMEM if i in smem else VMEM for i in range(count)],
        out_specs=jax.tree.map(lambda _: VMEM, outs),
        scratch_shapes=scratch,
        compiler_params=pltpu.CompilerParams(vmem_limit_bytes=40 << 20),
        cost_estimate=pl.CostEstimate(flops=flops, bytes_accessed=1 << 20, transcendentals=0),
        name=name,
    )


def per_device(factors, occ_energy, vir_energy, pair_code, pair_count):
    block = factors[0]
    vir, aux = block.shape
    width = vir // CHUNKS
    members, groups = lax.axis_size("mem"), lax.axis_size("grp")
    parts = [block[c * width : (c + 1) * width] for c in range(CHUNKS)]
    energy = occ_energy.astype(F32)
    row = vir_energy.astype(F32).reshape(1, vir)

    first = [turn(p, False) for p in parts]
    first_energy = turn(energy, False)

    shape = jax.ShapeDtypeStruct
    square = shape((vir, vir), F32)
    wide = shape((vir, aux), F32)
    dot = 2 * vir * vir * aux
    base, dens, gamma = call(
        early_kernel, (square, square, wide), [pltpu.VMEM((vir, vir), BF16)], (2, 3, 4), 5, 2 * dot, "early"
    )(block, row, energy, pair_code, pair_count)

    mts, ms = [], []
    for c in range(CHUNKS - 1):
        mt, m = call(
            functools.partial(part_kernel, c),
            (shape((vir, width), BF16), shape((width, vir), BF16)),
            (), (3, 4), 5, dot // CHUNKS, "part%d" % c,
        )(block, first[c], base, energy, first_energy)
        mts.append(mt)
        ms.append(m)
    old = [x for pair in zip(mts, ms) for x in pair]
    packed = len(blocks(vir)) * TILE
    half = packed // 2
    mt, _, keep, send = call(
        density_kernel,
        (shape((vir, width), BF16), shape((width, vir), BF16), shape((half, TILE), F32), shape((half, TILE), BF16)),
        [pltpu.VMEM((vir, vir), BF16), pltpu.VMEM((vir, vir), BF16), pltpu.VMEM((packed, TILE), F32)],
        (3, 4, 5, 6), 8 + len(old), dot // CHUNKS, "density",
    )(block, first[-1], base, energy, first_energy, pair_code, pair_count, dens, *old)
    mts.append(mt)

    total = keep + swap(send, 0, 1).astype(F32)
    total = total + swap(total.astype(BF16), 0, 3).astype(F32)
    bits = [1 << k for k in range(groups.bit_length() - 1)]
    for k, bit in enumerate(bits):
        twin = bits[k ^ 1] if (k ^ 1) < len(bits) else bit
        mask = functools.partial(lambda a, b, m: a if leads(m) else b, bit, twin)
        total = total + swap(total.astype(BF16), mask, 0).astype(F32)
    for k in range(2, members.bit_length() - 1):
        total = total + swap(total.astype(BF16), 0, (1 << k) | 3).astype(F32)
    mine = (total * (1.0 / (8.0 * groups * members))).astype(BF16)
    other = swap(mine, 0, 1)

    second = [turn(p, True) for p in parts]
    second_energy = turn(energy, True)
    gamma = call(first_gamma_kernel, wide, (), (0, 1), 3 + 2 * CHUNKS, dot, "gamma1")(
        pair_code, pair_count, gamma, *mts, *first
    )
    for c in range(CHUNKS):
        gamma = call(
            functools.partial(second_gamma_kernel, c),
            shape((vir, aux), F32 if c < CHUNKS - 1 else BF16),
            (), (0, 1, 5, 6), 8, 2 * dot // CHUNKS, "gamma2%d" % c,
        )(pair_code, pair_count, block, second[c], base, energy, second_energy, gamma)

    step = aux // CHUNKS
    lagrangian = pl.pallas_call(
        apply_kernel,
        out_shape=shape((vir, aux), BF16),
        grid=(CHUNKS,),
        in_specs=[
            pl.BlockSpec((half, TILE), lambda i: (0, 0)),
            pl.BlockSpec((half, TILE), lambda i: (0, 0)),
            pl.BlockSpec((vir, step), lambda i: (0, i)),
        ],
        out_specs=pl.BlockSpec((vir, step), lambda i: (0, i)),
        scratch_shapes=[pltpu.VMEM((vir, vir), BF16)],
        compiler_params=pltpu.CompilerParams(vmem_limit_bytes=24 << 20),
        cost_estimate=pl.CostEstimate(flops=dot, bytes_accessed=4 * vir * aux, transcendentals=0),
        name="apply",
    )(mine, other, block)
    return (gamma[None], lagrangian[None])


def solution(mesh):
    in_specs = (
        P(("grp", "mem"), None, None),
        P(("grp", "mem")),
        P(),
        P("grp", None, None),
        P("grp", None),
    )
    out_specs = (P(("grp", "mem"), None, None), P(("grp", "mem"), None, None))
    return jax.shard_map(
        per_device, mesh=mesh, in_specs=in_specs, out_specs=out_specs, check_vma=False
    )
```

time: 276 us -> 107 us (0.39)
  waiting for transfers between devices: 163 us -> 43.3 us
  Pallas kernels: 0 us -> 36.3 us
  local copies, waits for them, and re-layouts: 36.8 us -> 3.13 us
  matrix products: 32.8 us -> 0 us
  starting transfers between devices: 5.17 us -> 21.9 us
  other arithmetic: 14.5 us -> 0.3 us
  between operations: 14.7 us -> 1.49 us
  loops' own time: 8.85 us -> 0 us
    psum x2 -> x0, waiting for transfers between devices: 119 us -> none  [the longest x1 64.7 us: per_device(): density = lax.psum(density, 'mem')]
    pallas_call x0 -> x11, Pallas kernels: none -> 36.3 us  [the longest x4 15.4 us: per_device(): call(functools.partial(second_gamma_kernel, c), shape((vir, aux), F32 if...]
    dot_general x13 -> x0, matrix products: 32.8 us -> none  [the longest x3 18 us: pair_terms(): lax.dot_general(left_block, right_block, (((1,), (1,)), ((), ())), prefer...]
    while x18 -> x0, local copies, waits for them, and re-layouts: 17 us -> none
    ppermute x6 -> x16, starting transfers between devices: 5.09 us -> 21.9 us  [the longest x10 12.2 us: turn(): return lax.ppermute(value, 'mem', pairs)]
    another operation x1 -> x0, loops' own time: 8.85 us -> none  [per_device(): lax.fori_loop(0, live_count, pair_step, (density_zero, totals_zero))]
    convert_element_type x3 -> x5, other arithmetic: 9.01 us -> 0.3 us  [the longest x2 0.1 us: per_device(): total = total + swap(total.astype(BF16), mask, 0).astype(F32)]
    squeeze x1 -> x0, local copies, waits for them, and re-layouts: 8.24 us -> none  [per_device(): gathered = gathered + partner(totals[round_idx + 1], 'mem', round_idx)]
  transfers between devices with their start and end apart: 8 -> 16, of which waited for: 3 -> 6; matrix products, arithmetic and copies ran while one was open for 3% -> 0% of each run, Pallas kernels for 0% -> 27%
where the time goes in v1:
time: 107 us; the launch traced here: 106 us
  waiting for transfers between devices  43.3 us (40%)
  Pallas kernels  36.3 us (34%)
  starting transfers between devices  21.9 us (20%)
  local copies, waits for them, and re-layouts  3.13 us (3%)
  between operations  1.49 us (1%)
    ppermute x6, waiting for transfers between devices, swap(): return lax.ppermute(value, ('grp', 'mem'), pairs)  26.4 us
    ppermute x10, waiting for transfers between devices, turn(): return lax.ppermute(value, 'mem', pairs)  16.9 us
    pallas_call x4, Pallas kernels, per_device(): call(functools.partial(second_gamma_kernel, c), shape((vir, aux), F32 if...  15.4 us
    ppermute x10, starting transfers between devices, turn(): return lax.ppermute(value, 'mem', pairs)  12.2 us
    ppermute x6, starting transfers between devices, swap(): return lax.ppermute(value, ('grp', 'mem'), pairs)  9.65 us
    pallas_call x3, Pallas kernels, per_device(): call(functools.partial(part_kernel, c), (shape((vir, width), BF16), shape...  5.4 us
    pallas_call x1, Pallas kernels, per_device(): call(early_kernel, (square, square, wide), [pltpu.VMEM((vir, vir), BF16)]...  4.39 us
    pallas_call x1, Pallas kernels, per_device(): call(density_kernel, (shape((vir, width), BF16), shape((width, vir), BF16...  4.31 us
  transfers between devices with their start and end apart: 16, of which 6 were waited for; matrix products, arithmetic and copies ran while one was open for 0% of the time, Pallas kernels for 27%

profile of v1, /device:TPU:0, one launch (start us, length us, event | category | flops | bytes accessed | tf_op | source)
XLA Modules:
  0.0 106.4 jit_solution(12513113853695407469)
XLA Ops:
  0.6 0.0 copy-start
  0.7 3.0 %slice_bitcast_fusion = (bf16[128,2048]{1,0:T(8,128)(2,1)}, bf16[128,2048]{1,0:T(8,128)(2,1)}, bf16[128,2048]{1,0:T(8,128)(2,1)}, bf16[128,2048]{1,0:T(8,128)(2,1)}) fusion(bf16[1,512,2048]{2,1,0:T(8,128)(2,1)} %param.5), kind=kLoop, calls=%fused_computation | loop fusion | bytes 4194304 | tf_op jit(solution)/shard_map/slice | solution.py:196
  3.7 0.5 collective-permute-start.8
  4.2 2.1 %collective-permute-start.7 = (bf16[128,2048]{1,0:T(8,128)(2,1)}, bf16[128,2048]{1,0:T(8,128)(2,1)S(1)}, u32[]{:S(2)}, u32[]{:S(2)}) collective-permute-start(bf16[128,2048]{1,0:T(8,128)(2,1)} %get-tuple-element.31), channel_id=1, source_target_pairs={{0,1},{1,3},{2,0},{3,2},{4,5},{5,7},{6,4},{7,6},{8,9},{9,11},{10,8... | collective-permute-start | bytes 1572872 | tf_op jit(solution)/shard_map/ppermute | solution.py:32
  6.3 0.7 collective-permute-start.5
  7.0 0.0 collective-permute-start.9
  7.7 2.0 %collective-permute-start.6 = (f32[1]{0:T(128)}, f32[1]{0:T(128)}, u32[]{:S(2)}, u32[]{:S(2)}) collective-permute-start(f32[1]{0:T(128)} %convert_element_type.34.e_ref.refs_3_), channel_id=1, source_target_pairs={{0,1},{1,3},{2,0},{3,2},{4,5},{5,7},{6,4},{7,6},{8,9},{9,11},{10,8... | collective-permute-start | bytes 20 | tf_op jit(solution)/shard_map/ppermute | solution.py:32
  9.7 0.1 copy.13.codes.refs_5_.refs_0_
  9.8 4.4 %early.1 = (f32[512,512]{1,0:T(8,128)S(1)}, f32[512,512]{1,0:T(8,128)S(1)}, f32[512,2048]{1,0:T(8,128)S(1)}) custom-call(bf16[512,2048]{1,0:T(8,128)(2,1)S(1)} %bitcast.12, f32[1,512]{1,0:T(1,128)S(1)} %bitcast.22, f32[1]{0:T(128)} %convert_element_type.34.e_ref.refs_3_, s32[1,8,3]{2,1,0:T(8,128)S(1)} %copy.13.codes.refs_5_.refs_0_, s32[1,8]{1,0:T(1,128)S(1)} %copy-done.1), custom_call_target="tpu_custom_call" | custom-call | flops 2147483648 | bytes 1048576 | tf_op jit(solution)/shard_map/early/pallas_call | solution.py:207
  14.2 16.9 %collective-permute-done.6.far_ref.refs_4_ = f32[1]{0:T(128)} collective-permute-done((f32[1]{0:T(128)}, f32[1]{0:T(128)}, u32[]{:S(2)}, u32[]{:S(2)}) %collective-permute-start.6) | collective-permute-done | bytes 36 | tf_op jit(solution)/shard_map/ppermute | solution.py:32
  31.1 0.0 collective-permute-done.8.r_ref.refs_9_
  31.1 1.5 %part2.1 = (bf16[512,128]{1,0:T(8,128)(2,1)S(1)}, bf16[128,512]{1,0:T(8,128)(2,1)S(1)}) custom-call(bf16[512,2048]{1,0:T(8,128)(2,1)S(1)} %bitcast.13, bf16[128,2048]{1,0:T(8,128)(2,1)S(1)} %collective-permute-done.8.r_ref.refs_9_, f32[512,512]{1,0:T(8,128)S(1)} %get-tuple-element.14.base_ref.refs_2_, f32[1]{0:T(128)} %convert_element_type.34.e_ref.refs_3_, ...), custom_call_target="tpu_custom_call" | custom-call | flops 268435456 | bytes 1048576 | tf_op jit(solution)/shard_map/part2/pallas_call | solution.py:213
  32.5 0.0 collective-permute-done.7.r_ref.refs_8_
  32.6 1.5 %part1.1 = (bf16[512,128]{1,0:T(8,128)(2,1)S(1)}, bf16[128,512]{1,0:T(8,128)(2,1)S(1)}) custom-call(bf16[512,2048]{1,0:T(8,128)(2,1)S(1)} %bitcast.14, bf16[128,2048]{1,0:T(8,128)(2,1)S(1)} %collective-permute-done.7.r_ref.refs_8_, f32[512,512]{1,0:T(8,128)S(1)} %get-tuple-element.14.base_ref.refs_2_, f32[1]{0:T(128)} %convert_element_type.34.e_ref.refs_3_, ...), custom_call_target="tpu_custom_call" | custom-call | flops 268435456 | bytes 1048576 | tf_op jit(solution)/shard_map/part1/pallas_call | solution.py:213
  34.0 0.0 collective-permute-done.5.r_ref.refs_7_
  34.0 2.5 %part0.1 = (bf16[512,128]{1,0:T(8,128)(2,1)S(1)}, bf16[128,512]{1,0:T(8,128)(2,1)S(1)}) custom-call(bf16[512,2048]{1,0:T(8,128)(2,1)S(1)} %bitcast.15, bf16[128,2048]{1,0:T(8,128)(2,1)} %collective-permute-done.5.r_ref.refs_7_, f32[512,512]{1,0:T(8,128)S(1)} %get-tuple-element.14.base_ref.refs_2_, f32[1]{0:T(128)} %convert_element_type.34.e_ref.refs_3_, ...), custom_call_target="tpu_custom_call" | custom-call | flops 268435456 | bytes 1048576 | tf_op jit(solution)/shard_map/part0/pallas_call | solution.py:213
  36.5 0.0 collective-permute-done.9.refs_1_.refs_10_
  36.5 4.3 %density.1 = (bf16[512,128]{1,0:T(8,128)(2,1)S(1)}, bf16[128,512]{1,0:T(8,128)(2,1)}, f32[640,128]{1,0:T(8,128)S(1)}, bf16[640,128]{1,0:T(8,128)(2,1)S(1)}) custom-call(bf16[512,2048]{1,0:T(8,128)(2,1)S(1)} %bitcast.16, bf16[128,2048]{1,0:T(8,128)(2,1)} %collective-permute-done.9.refs_1_.refs_10_, f32[512,512]{1,0:T(8,128)S(1)} %get-tuple-element.14.base_ref.refs_2_, ...), custom_call_target="tpu_custom_call" | custom-call | flops 268435456 | bytes 1048576 | tf_op jit(solution)/shard_map/density/pallas_call | solution.py:223
  40.8 3.0 %collective-permute-start.10 = (bf16[640,128]{1,0:T(8,128)(2,1)S(1)}, bf16[640,128]{1,0:T(8,128)(2,1)S(1)}, u32[]{:S(2)}, u32[]{:S(2)}) collective-permute-start(bf16[640,128]{1,0:T(8,128)(2,1)S(1)} %get-tuple-element.25), channel_id=1, source_target_pairs={{0,1},{1,0},{2,3},{3,2},{4,5},{5,4},{6,7},{7,6},{8,9},{9,8},{10,11... | collective-permute-start | bytes 491528 | tf_op jit(solution)/shard_map/ppermute | solution.py:42
  43.9 1.0 collective-permute-done.10
  45.0 1.2 %collective-permute-start.11 = (bf16[640,128]{1,0:T(8,128)(2,1)S(1)}, bf16[640,128]{1,0:T(8,128)(2,1)S(1)}, u32[]{:S(2)}, u32[]{:S(2)}) collective-permute-start(bf16[640,128]{1,0:T(8,128)(2,1)S(1)} %fusion), channel_id=1, source_target_pairs={{0,3},{1,2},{2,1},{3,0},{4,7},{5,6},{6,5},{7,4},{8,11},{9,10},{10,... | collective-permute-start | bytes 491528 | tf_op jit(solution)/shard_map/ppermute | solution.py:42
  46.2 4.8 %collective-permute-done.11 = bf16[640,128]{1,0:T(8,128)(2,1)S(1)} collective-permute-done((bf16[640,128]{1,0:T(8,128)(2,1)S(1)}, bf16[640,128]{1,0:T(8,128)(2,1)S(1)}, u32[]{:S(2)}, u32[]{:S(2)}) %collective-permute-start.11) | collective-permute-done | bytes 163872 | tf_op jit(solution)/shard_map/ppermute | solution.py:42
  51.0 0.1 fusion.3
  51.0 1.6 %collective-permute-start.12 = (bf16[640,128]{1,0:T(8,128)(2,1)S(1)}, bf16[640,128]{1,0:T(8,128)(2,1)S(1)}, u32[]{:S(2)}, u32[]{:S(2)}) collective-permute-start(bf16[640,128]{1,0:T(8,128)(2,1)S(1)} %get-tuple-element.26), channel_id=1, source_target_pairs={{0,8},{1,17},{2,18},{3,11},{4,12},{5,21},{6,22},{7,15},{8,0},{9,25... | collective-permute-start | bytes 491528 | tf_op jit(solution)/shard_map/ppermute | solution.py:42
  52.6 3.8 %collective-permute-done.12 = bf16[640,128]{1,0:T(8,128)(2,1)S(1)} collective-permute-done((bf16[640,128]{1,0:T(8,128)(2,1)S(1)}, bf16[640,128]{1,0:T(8,128)(2,1)S(1)}, u32[]{:S(2)}, u32[]{:S(2)}) %collective-permute-start.12) | collective-permute-done | bytes 163872 | tf_op jit(solution)/shard_map/ppermute | solution.py:42
  56.5 1.6 %collective-permute-start.13 = (bf16[640,128]{1,0:T(8,128)(2,1)S(1)}, bf16[640,128]{1,0:T(8,128)(2,1)S(1)}, u32[]{:S(2)}, u32[]{:S(2)}) collective-permute-start(bf16[640,128]{1,0:T(8,128)(2,1)S(1)} %fusion.1), channel_id=1, source_target_pairs={{0,16},{1,9},{2,10},{3,19},{4,20},{5,13},{6,14},{7,23},{8,24},{9,1... | collective-permute-start | bytes 491528 | tf_op jit(solution)/shard_map/ppermute | solution.py:42
  58.1 2.0 %collective-permute-start.4 = (bf16[128,2048]{1,0:T(8,128)(2,1)}, bf16[128,2048]{1,0:T(8,128)(2,1)S(1)}, u32[]{:S(2)}, u32[]{:S(2)}) collective-permute-start(bf16[128,2048]{1,0:T(8,128)(2,1)} %get-tuple-element.28), channel_id=1, source_target_pairs={{1,0},{3,1},{0,2},{2,3},{5,4},{7,5},{4,6},{6,7},{9,8},{11,9},{8,10... | collective-permute-start | bytes 1572872 | tf_op jit(solution)/shard_map/ppermute | solution.py:32
  60.1 0.0 collective-permute-start.2
  60.1 0.0 collective-permute-start.3
  60.1 1.7 %collective-permute-done.13 = bf16[640,128]{1,0:T(8,128)(2,1)S(1)} collective-permute-done((bf16[640,128]{1,0:T(8,128)(2,1)S(1)}, bf16[640,128]{1,0:T(8,128)(2,1)S(1)}, u32[]{:S(2)}, u32[]{:S(2)}) %collective-permute-start.13) | collective-permute-done | bytes 163872 | tf_op jit(solution)/shard_map/ppermute | solution.py:42
  61.8 0.1 fusion.2
  61.9 2.2 %collective-permute-start.14 = (bf16[640,128]{1,0:T(8,128)(2,1)S(1)}, bf16[640,128]{1,0:T(8,128)(2,1)S(1)}, u32[]{:S(2)}, u32[]{:S(2)}) collective-permute-start(bf16[640,128]{1,0:T(8,128)(2,1)S(1)} %fusion.2), channel_id=1, source_target_pairs={{0,7},{1,6},{2,5},{3,4},{4,3},{5,2},{6,1},{7,0},{8,15},{9,14},{10,... | collective-permute-start | bytes 491528 | tf_op jit(solution)/shard_map/ppermute | solution.py:42
  64.1 0.0 collective-permute-start
  64.1 3.5 %gamma1.1.gamma_in = f32[512,2048]{1,0:T(8,128)S(1)} custom-call(s32[1,8,3]{2,1,0:T(8,128)S(1)} %copy.13.codes.refs_5_.refs_0_, s32[1,8]{1,0:T(1,128)S(1)} %copy-done.1, f32[512,2048]{1,0:T(8,128)S(1)} %get-tuple-element.15.refs_2_, bf16[512,128]{1,0:T(8,128)(2,1)S(1)} %get-tuple-element.16.refs_8_.refs_3_, ...), custom_call_target="tpu_custom_call" | custom-call | flops 1073741824 | bytes 1048576 | tf_op jit(solution)/shard_map/gamma1/pallas_call | solution.py:245
  67.7 15.0 %collective-permute-done.14 = bf16[640,128]{1,0:T(8,128)(2,1)S(1)} collective-permute-done((bf16[640,128]{1,0:T(8,128)(2,1)S(1)}, bf16[640,128]{1,0:T(8,128)(2,1)S(1)}, u32[]{:S(2)}, u32[]{:S(2)}) %collective-permute-start.14) | collective-permute-done | bytes 163872 | tf_op jit(solution)/shard_map/ppermute | solution.py:42
  82.7 4.8 %collective-permute-start.1 = (f32[1]{0:T(128)}, f32[1]{0:T(128)}, u32[]{:S(2)}, u32[]{:S(2)}) collective-permute-start(f32[1]{0:T(128)} %convert_element_type.34.e_ref.refs_3_), channel_id=1, source_target_pairs={{1,0},{3,1},{0,2},{2,3},{5,4},{7,5},{4,6},{6,7},{9,8},{11,9},{8,10... | collective-permute-start | bytes 20 | tf_op jit(solution)/shard_map/ppermute | solution.py:32
  87.5 0.1 multiply_convert_fusion.mine_ref
  87.6 0.1 collective-permute-start.15
  87.7 0.0 collective-permute-done.4.r_ref
  87.7 3.5 %gamma20.1.gamma_in = f32[512,2048]{1,0:T(8,128)S(1)} custom-call(s32[1,8,3]{2,1,0:T(8,128)S(1)} %copy.13.codes.refs_5_.refs_0_, s32[1,8]{1,0:T(1,128)S(1)} %copy-done.1, bf16[512,2048]{1,0:T(8,128)(2,1)S(1)} %bitcast.17, bf16[128,2048]{1,0:T(8,128)(2,1)S(1)} %collective-permute-done.4.r_ref, f32[512,512]{1,0:T(8,128)S(1)} %get-tuple-element.14.base_ref.refs_2_, ...), custom_call_target="tpu_custom_call" | custom-call | flops 536870912 | bytes 1048576 | tf_op jit(solution)/shard_map/gamma20/pallas_call | solution.py:249
  91.2 0.0 collective-permute-done.3.r_ref
  91.2 3.5 %gamma21.1.gamma_in = f32[512,2048]{1,0:T(8,128)S(1)} custom-call(s32[1,8,3]{2,1,0:T(8,128)S(1)} %copy.13.codes.refs_5_.refs_0_, s32[1,8]{1,0:T(1,128)S(1)} %copy-done.1, bf16[512,2048]{1,0:T(8,128)(2,1)S(1)} %bitcast.18, bf16[128,2048]{1,0:T(8,128)(2,1)S(1)} %collective-permute-done.3.r_ref, f32[512,512]{1,0:T(8,128)S(1)} %get-tuple-element.14.base_ref.refs_2_, ...), custom_call_target="tpu_custom_call" | custom-call | flops 536870912 | bytes 1048576 | tf_op jit(solution)/shard_map/gamma21/pallas_call | solution.py:249
  94.7 0.0 collective-permute-done.2.r_ref
  94.8 3.5 %gamma22.1.gamma_in = f32[512,2048]{1,0:T(8,128)S(1)} custom-call(s32[1,8,3]{2,1,0:T(8,128)S(1)} %copy.13.codes.refs_5_.refs_0_, s32[1,8]{1,0:T(1,128)S(1)} %copy-done.1, bf16[512,2048]{1,0:T(8,128)(2,1)S(1)} %bitcast.19, bf16[128,2048]{1,0:T(8,128)(2,1)S(1)} %collective-permute-done.2.r_ref, f32[512,512]{1,0:T(8,128)S(1)} %get-tuple-element.14.base_ref.refs_2_, ...), custom_call_target="tpu_custom_call" | custom-call | flops 536870912 | bytes 1048576 | tf_op jit(solution)/shard_map/gamma22/pallas_call | solution.py:249
  98.3 0.0 collective-permute-done.r_ref
  98.3 4.8 %gamma23.1 = bf16[512,2048]{1,0:T(8,128)(2,1)} custom-call(s32[1,8,3]{2,1,0:T(8,128)S(1)} %copy.13.codes.refs_5_.refs_0_, s32[1,8]{1,0:T(1,128)S(1)} %copy-done.1, bf16[512,2048]{1,0:T(8,128)(2,1)S(1)} %bitcast.20, bf16[128,2048]{1,0:T(8,128)(2,1)S(1)} %collective-permute-done.r_ref, f32[512,512]{1,0:T(8,128)S(1)} %get-tuple-element.14.base_ref.refs_2_, ...), custom_call_target="tpu_custom_call" | custom-call | flops 536870912 | bytes 1048576 | tf_op jit(solution)/shard_map/gamma23/pallas_call | solution.py:249
  103.1 0.0 collective-permute-done.15.other_ref
  103.1 3.2 %apply.1 = bf16[512,2048]{1,0:T(8,128)(2,1)} custom-call(bf16[640,128]{1,0:T(8,128)(2,1)S(1)} %multiply_convert_fusion.mine_ref, bf16[640,128]{1,0:T(8,128)(2,1)S(1)} %collective-permute-done.15.other_ref, bf16[512,2048]{1,0:T(8,128)(2,1)S(1)} %bitcast.21), custom_call_target="tpu_custom_call" | custom-call | flops 1073741824 | bytes 4194304 | tf_op jit(solution)/shard_map/apply/pallas_call | solution.py:256
  (11 shorter events, 0.1 us)
Async XLA Ops:
  0.6 9.2 %copy-start = (bf16[1,512,2048]{2,1,0:T(8,128)(2,1)S(1)}, bf16[1,512,2048]{2,1,0:T(8,128)(2,1)}, u32[]{:S(2)}) copy-start(bf16[1,512,2048]{2,1,0:T(8,128)(2,1)} %param.5) | copy-start | bytes 6291460
  0.6 9.1 %copy-start.3 = (bf16[512]{0:T(512)(128)(2,1)S(1)}, bf16[512]{0:T(512)(128)(2,1)}, u32[]{:S(2)}) copy-start(bf16[512]{0:T(512)(128)(2,1)} %param.7) | copy-start | bytes 3076
  0.7 9.0 %copy-start.2 = (s32[1,8,3]{1,0,2:T(1,128)S(1)}, s32[1,8,3]{1,0,2:T(1,128)}, u32[]{:S(2)}) copy-start(s32[1,8,3]{1,0,2:T(1,128)} %param.8) | copy-start | bytes 292
  0.7 9.1 %copy-start.1 = (s32[1,8]{1,0:T(1,128)S(1)}, s32[1,8]{1,0:T(1,128)}, u32[]{:S(2)}) copy-start(s32[1,8]{1,0:T(1,128)} %counts.9) | copy-start | bytes 100
  3.7 27.4 %collective-permute-start.8 = (bf16[128,2048]{1,0:T(8,128)(2,1)}, bf16[128,2048]{1,0:T(8,128)(2,1)S(1)}, u32[]{:S(2)}, u32[]{:S(2)}) collective-permute-start(bf16[128,2048]{1,0:T(8,128)(2,1)} %get-tuple-element.29), channel_id=1, source_target_pairs={{0,1},{1,3},{2,0},{3,2},{4,5},{5,7},{6,4},{7,6},{8,9},{9,11},{10,8... | collective-permute-start | bytes 1572872 | tf_op jit(solution)/shard_map/ppermute | solution.py:32
  4.2 28.4 %collective-permute-start.7 = (bf16[128,2048]{1,0:T(8,128)(2,1)}, bf16[128,2048]{1,0:T(8,128)(2,1)S(1)}, u32[]{:S(2)}, u32[]{:S(2)}) collective-permute-start(bf16[128,2048]{1,0:T(8,128)(2,1)} %get-tuple-element.31), channel_id=1, source_target_pairs={{0,1},{1,3},{2,0},{3,2},{4,5},{5,7},{6,4},{7,6},{8,9},{9,11},{10,8... | collective-permute-start | bytes 1572872 | tf_op jit(solution)/shard_map/ppermute | solution.py:32
  6.3 27.7 %collective-permute-start.5 = (bf16[128,2048]{1,0:T(8,128)(2,1)}, bf16[128,2048]{1,0:T(8,128)(2,1)}, u32[]{:S(2)}, u32[]{:S(2)}) collective-permute-start(bf16[128,2048]{1,0:T(8,128)(2,1)} %get-tuple-element.28), channel_id=1, source_target_pairs={{0,1},{1,3},{2,0},{3,2},{4,5},{5,7},{6,4},{7,6},{8,9},{9,11},{10,8... | collective-permute-start | bytes 1572872 | tf_op jit(solution)/shard_map/ppermute | solution.py:32
  7.0 29.5 %collective-permute-start.9 = (bf16[128,2048]{1,0:T(8,128)(2,1)}, bf16[128,2048]{1,0:T(8,128)(2,1)}, u32[]{:S(2)}, u32[]{:S(2)}) collective-permute-start(bf16[128,2048]{1,0:T(8,128)(2,1)} %get-tuple-element.30), channel_id=1, source_target_pairs={{0,1},{1,3},{2,0},{3,2},{4,5},{5,7},{6,4},{7,6},{8,9},{9,11},{10,8... | collective-permute-start | bytes 1572872 | tf_op jit(solution)/shard_map/ppermute | solution.py:32
  7.7 23.4 %collective-permute-start.6 = (f32[1]{0:T(128)}, f32[1]{0:T(128)}, u32[]{:S(2)}, u32[]{:S(2)}) collective-permute-start(f32[1]{0:T(128)} %convert_element_type.34.e_ref.refs_3_), channel_id=1, source_target_pairs={{0,1},{1,3},{2,0},{3,2},{4,5},{5,7},{6,4},{7,6},{8,9},{9,11},{10,8... | collective-permute-start | bytes 20 | tf_op jit(solution)/shard_map/ppermute | solution.py:32
  40.8 4.1 %collective-permute-start.10 = (bf16[640,128]{1,0:T(8,128)(2,1)S(1)}, bf16[640,128]{1,0:T(8,128)(2,1)S(1)}, u32[]{:S(2)}, u32[]{:S(2)}) collective-permute-start(bf16[640,128]{1,0:T(8,128)(2,1)S(1)} %get-tuple-element.25), channel_id=1, source_target_pairs={{0,1},{1,0},{2,3},{3,2},{4,5},{5,4},{6,7},{7,6},{8,9},{9,8},{10,11... | collective-permute-start | bytes 491528 | tf_op jit(solution)/shard_map/ppermute | solution.py:42
  45.0 6.0 %collective-permute-start.11 = (bf16[640,128]{1,0:T(8,128)(2,1)S(1)}, bf16[640,128]{1,0:T(8,128)(2,1)S(1)}, u32[]{:S(2)}, u32[]{:S(2)}) collective-permute-start(bf16[640,128]{1,0:T(8,128)(2,1)S(1)} %fusion), channel_id=1, source_target_pairs={{0,3},{1,2},{2,1},{3,0},{4,7},{5,6},{6,5},{7,4},{8,11},{9,10},{10,... | collective-permute-start | bytes 491528 | tf_op jit(solution)/shard_map/ppermute | solution.py:42
  51.0 5.4 %collective-permute-start.12 = (bf16[640,128]{1,0:T(8,128)(2,1)S(1)}, bf16[640,128]{1,0:T(8,128)(2,1)S(1)}, u32[]{:S(2)}, u32[]{:S(2)}) collective-permute-start(bf16[640,128]{1,0:T(8,128)(2,1)S(1)} %get-tuple-element.26), channel_id=1, source_target_pairs={{0,8},{1,17},{2,18},{3,11},{4,12},{5,21},{6,22},{7,15},{8,0},{9,25... | collective-permute-start | bytes 491528 | tf_op jit(solution)/shard_map/ppermute | solution.py:42
  56.5 5.4 %collective-permute-start.13 = (bf16[640,128]{1,0:T(8,128)(2,1)S(1)}, bf16[640,128]{1,0:T(8,128)(2,1)S(1)}, u32[]{:S(2)}, u32[]{:S(2)}) collective-permute-start(bf16[640,128]{1,0:T(8,128)(2,1)S(1)} %fusion.1), channel_id=1, source_target_pairs={{0,16},{1,9},{2,10},{3,19},{4,20},{5,13},{6,14},{7,23},{8,24},{9,1... | collective-permute-start | bytes 491528 | tf_op jit(solution)/shard_map/ppermute | solution.py:42
  58.1 29.6 %collective-permute-start.4 = (bf16[128,2048]{1,0:T(8,128)(2,1)}, bf16[128,2048]{1,0:T(8,128)(2,1)S(1)}, u32[]{:S(2)}, u32[]{:S(2)}) collective-permute-start(bf16[128,2048]{1,0:T(8,128)(2,1)} %get-tuple-element.28), channel_id=1, source_target_pairs={{1,0},{3,1},{0,2},{2,3},{5,4},{7,5},{4,6},{6,7},{9,8},{11,9},{8,10... | collective-permute-start | bytes 1572872 | tf_op jit(solution)/shard_map/ppermute | solution.py:32
  60.1 34.7 %collective-permute-start.2 = (bf16[128,2048]{1,0:T(8,128)(2,1)}, bf16[128,2048]{1,0:T(8,128)(2,1)S(1)}, u32[]{:S(2)}, u32[]{:S(2)}) collective-permute-start(bf16[128,2048]{1,0:T(8,128)(2,1)} %get-tuple-element.29), channel_id=1, source_target_pairs={{1,0},{3,1},{0,2},{2,3},{5,4},{7,5},{4,6},{6,7},{9,8},{11,9},{8,10... | collective-permute-start | bytes 1572872 | tf_op jit(solution)/shard_map/ppermute | solution.py:32
  60.1 31.1 %collective-permute-start.3 = (bf16[128,2048]{1,0:T(8,128)(2,1)}, bf16[128,2048]{1,0:T(8,128)(2,1)S(1)}, u32[]{:S(2)}, u32[]{:S(2)}) collective-permute-start(bf16[128,2048]{1,0:T(8,128)(2,1)} %get-tuple-element.31), channel_id=1, source_target_pairs={{1,0},{3,1},{0,2},{2,3},{5,4},{7,5},{4,6},{6,7},{9,8},{11,9},{8,10... | collective-permute-start | bytes 1572872 | tf_op jit(solution)/shard_map/ppermute | solution.py:32
  61.9 20.8 %collective-permute-start.14 = (bf16[640,128]{1,0:T(8,128)(2,1)S(1)}, bf16[640,128]{1,0:T(8,128)(2,1)S(1)}, u32[]{:S(2)}, u32[]{:S(2)}) collective-permute-start(bf16[640,128]{1,0:T(8,128)(2,1)S(1)} %fusion.2), channel_id=1, source_target_pairs={{0,7},{1,6},{2,5},{3,4},{4,3},{5,2},{6,1},{7,0},{8,15},{9,14},{10,... | collective-permute-start | bytes 491528 | tf_op jit(solution)/shard_map/ppermute | solution.py:42
  64.1 34.2 %collective-permute-start = (bf16[128,2048]{1,0:T(8,128)(2,1)}, bf16[128,2048]{1,0:T(8,128)(2,1)S(1)}, u32[]{:S(2)}, u32[]{:S(2)}) collective-permute-start(bf16[128,2048]{1,0:T(8,128)(2,1)} %get-tuple-element.30), channel_id=1, source_target_pairs={{1,0},{3,1},{0,2},{2,3},{5,4},{7,5},{4,6},{6,7},{9,8},{11,9},{8,10... | collective-permute-start | bytes 1572872 | tf_op jit(solution)/shard_map/ppermute | solution.py:32
  82.7 4.9 %collective-permute-start.1 = (f32[1]{0:T(128)}, f32[1]{0:T(128)}, u32[]{:S(2)}, u32[]{:S(2)}) collective-permute-start(f32[1]{0:T(128)} %convert_element_type.34.e_ref.refs_3_), channel_id=1, source_target_pairs={{1,0},{3,1},{0,2},{2,3},{5,4},{7,5},{4,6},{6,7},{9,8},{11,9},{8,10... | collective-permute-start | bytes 20 | tf_op jit(solution)/shard_map/ppermute | solution.py:32
  87.6 15.6 %collective-permute-start.15 = (bf16[640,128]{1,0:T(8,128)(2,1)S(1)}, bf16[640,128]{1,0:T(8,128)(2,1)S(1)}, u32[]{:S(2)}, u32[]{:S(2)}) collective-permute-start(bf16[640,128]{1,0:T(8,128)(2,1)S(1)} %multiply_convert_fusion.mine_ref), channel_id=1, source_target_pairs={{0,1},{1,0},{2,3},{3,2},{4,5},{5,4},{6,7},{7,6},{8,9},{9,8},{10,11... | collective-permute-start | bytes 491528 | tf_op jit(solution)/shard_map/ppermute | solution.py:42
